TPU v7x, 256 devices: a whole 4x4x8 slice. The times are simulated.
256 devices in a mesh: row: 64 (over y, z, core), col: 4 (over x).
Axes of the slice: x: 4, y: 4, z: 8, core: 2. Of those that a mesh axis runs over, the one named last changes fastest.
Arguments:
- trailing: float32 [65536, 4096], P('row', 'col'), may hold values from -6 to 6
- panel_y: float32 [65536, 256], P(('row', 'col')), may hold values from -0.1875 to 0.1875
- panel_t: float32 [16384, 256], P('row'), may hold values from 0.5 to 1.5
- tree_v: float32 [3, 16384, 256], P(None, 'row'), may hold values from -0.375 to 0.375, as said below
- tree_t: float32 [3, 16384, 256], P(None, 'row'), may hold values from 0.5 to 1.5, as said below
Outputs:
- updated: float32 [65536, 4096], P('row', 'col')
Inputs may be any that keep to these rules, and one draw needn't show every extreme that they name: For each level l, the blocks of 256 rows that tree_v[l] holds for two tile rows that differ only in bit l are equal. For each level l, the blocks of 256 rows that tree_t[l] holds for two tile rows that differ only in bit l are equal.
All inputs are finite; a program needn't handle non-finite values.
Results may differ from a plain program's by a relative error of at most 0.0001.
Values sent between devices are 32-bit elements; how exact they have to be, the bound alone decides.
No kernel may reach another device: no remote copies, remote signals or barrier semaphores. Data moves between devices by JAX's collectives and lax.ppermute only.
A program may use at most 64 MiB of HBM per device.

v0:
```python
import math
import jax
import jax.numpy as jnp
from jax import lax
from jax.sharding import PartitionSpec as P


def from_partner(block, axis, bit):
    count = lax.axis_size(axis)
    route = []
    for low in range(count):
        high = low | 1 << bit
        if high != low and high < count:
            route += [(low, high), (high, low)]
    return lax.ppermute(block, axis, route)


def unit_lower(values):
    rows = jnp.arange(values.shape[0])[:, None]
    cols = jnp.arange(values.shape[1])[None, :]
    return jnp.where(
        rows > cols, values, jnp.where(rows == cols, jnp.float32(1.0), jnp.float32(0.0))
    )


def triangle_factor(values):
    width = values.shape[-1]
    rows = jnp.arange(width)[:, None]
    cols = jnp.arange(width)[None, :]
    scale = 2.0 / math.sqrt(width)
    return jnp.where(
        rows == cols, values, jnp.where(cols > rows, (values - 1.0) * scale, jnp.float32(0.0))
    )


def upper_part(values):
    width = values.shape[-1]
    rows = jnp.arange(width)[:, None]
    cols = jnp.arange(width)[None, :]
    return jnp.where(cols >= rows, values, jnp.float32(0.0))


def pair_update(first, second, vees, tees):
    highest = lax.Precision.HIGHEST
    summed = first + jnp.einsum("kb,kn->bn", vees, second, precision=highest)
    factor = jnp.einsum("kb,kn->bn", tees, summed, precision=highest)
    return (first - factor, second - jnp.dot(vees, factor, precision=highest))


def per_device(trailing, panel_y, panel_t, tree_v, tree_t):
    highest = lax.Precision.HIGHEST
    width = panel_t.shape[1]
    columns = trailing.shape[1]
    half = columns // 2
    gathered = lax.all_gather(panel_y, "col", axis=0, tiled=True)
    lower = unit_lower(gathered)
    proj = jnp.einsum("mb,mn->bn", lower, trailing, precision=highest)
    weight = jnp.einsum("kb,kn->bn", triangle_factor(panel_t), proj, precision=highest)
    local = trailing - jnp.dot(lower, weight, precision=highest)
    top = local[:width]
    rest = local[width:]
    position = lax.axis_index("row")
    for level in range(tree_v.shape[0]):
        leader = position >> level & 1 == 0
        vees = upper_part(tree_v[level])
        tees = triangle_factor(tree_t[level])
        left = top[:, :half]
        right = top[:, half:]
        outgoing = jnp.where(leader, right, left)
        incoming = from_partner(outgoing, "row", level)
        first = jnp.where(leader, left, incoming)
        second = jnp.where(leader, incoming, right)
        new_first, new_second = pair_update(first, second, vees, tees)
        sendback = jnp.where(leader, new_second, new_first)
        returned = from_partner(sendback, "row", level)
        top = jnp.where(
            leader,
            jnp.concatenate([new_first, returned], axis=1),
            jnp.concatenate([returned, new_second], axis=1),
        )
    return jnp.concatenate([top, rest], axis=0)


def solution(mesh):
    placed = (
        P("row", "col"),
        P(("row", "col"), None),
        P("row", None),
        P(None, "row", None),
        P(None, "row", None),
    )
    return jax.shard_map(
        per_device, mesh=mesh, in_specs=placed, out_specs=P("row", "col"), check_vma=False
    )
```

profile of v0, /device:TPU:8, one launch (start us, length us, event | category | flops | bytes accessed | tf_op | source)
XLA Modules:
  0.0 161.7 jit_solution(15290932979044176380)
XLA Ops:
  6.5 0.0 all-gather.2.cloned.1.call-start
  6.5 0.7 all-gather.2.cloned.1.call-update
  7.3 5.3 %copy.6 = f32[1024,1024]{0,1:T(8,128)} copy(f32[1024,1024]{1,0:T(8,128)} %param.5) | data formatting | bytes 8388608 | tf_op args[0]
  12.6 26.1 %all-gather.2.cloned.1.call-done = f32[1024,256]{1,0:T(8,128)} async-done(((f32[256,256]{1,0:T(8,128)}), f32[1024,256]{1,0:T(8,128)}) %all-gather.2.cloned.1.call-update) | async-done | bytes 1048592 | tf_op jit(solution)/shard_map/all_gather | solution.py:55
  38.7 6.0 %fusion = f32[256,1024]{1,0:T(8,128)S(1)} fusion(f32[1024,1024]{1,0:T(8,128)} %param.5, f32[1024,256]{1,0:T(8,128)} %all-gather.2.cloned.1.call-done), kind=kOutput, calls=%fused_computation.14 | convolution fusion | flops 3222274048 | bytes 6291456 | tf_op jit(solution)/shard_map/mb,mn->bn/dot_general | solution.py:57
  44.7 0.0 copy-done.4
  44.7 1.1 fusion.17
  45.8 0.0 copy-done.1
  45.8 0.0 copy-done.2
  45.8 0.0 copy-start.3
  45.8 3.8 %convolution_subtract_fusion = f32[1024,1024]{0,1:T(8,128)S(1)} fusion(f32[1024,1024]{0,1:T(8,128)S(1)} %copy-done.1, f32[256,1024]{1,0:T(8,128)S(1)} %fusion.17, f32[1024,256]{1,0:T(8,128)S(1)} %copy-done.2), kind=kOutput, calls=%fused_computation.1 | convolution fusion | flops 3223322624 | bytes 10485760 | tf_op jit(solution)/shard_map/dot_general | solution.py:59
  49.6 0.0 copy-start
  49.6 0.1 slice_select_fusion.7
  49.8 0.1 collective-permute-start
  49.9 1.9 %collective-permute-done = f32[256,512]{0,1:T(8,128)S(1)} collective-permute-done((f32[256,512]{0,1:T(8,128)S(1)}, f32[256,512]{0,1:T(8,128)S(1)}, u32[]{:S(2)}, u32[]{:S(2)}) %collective-permute-start) | collective-permute-done | bytes 524320 | tf_op jit(solution)/shard_map/ppermute | solution.py:15
  51.8 0.0 copy-done
  51.8 0.0 copy-done.3
  51.8 0.6 convolution_add_fusion.2
  52.4 1.8 %fusion.13 = f32[256,512]{1,0:T(8,128)S(1)} fusion(f32[256,512]{0,1:T(8,128)S(1)} %convolution_add_fusion.2, f32[3,256,256]{2,1,0:T(8,128)} %param.9), kind=kOutput, calls=%fused_computation.45 | convolution fusion | flops 403046400 | bytes 1310720 | tf_op jit(solution)/shard_map/kb,kn->bn/dot_general | solution.py:46
  54.3 0.2 copy.7
  54.5 3.0 %broadcast_select_fusion = (f32[256,512]{0,1:T(8,128)}, f32[256,512]{0,1:T(8,128)S(1)}, f32[256,512]{0,1:T(8,128)S(1)}) fusion(pred[]{:T(512)S(6)} %eq.100, f32[256,512]{0,1:T(8,128)S(1)} %copy.7, f32[256,512]{0,1:T(8,128)S(1)} %collective-permute-done, f32[1024,1024]{0,1:T(8,128)} %copy-done, f32[256,512]{1,0:T(8,128)S(1)} %fusion.13, ...), kind=kOutput, calls=%fused_computation.57 | convolution fusion | flops 403439616 | bytes 4456449 | tf_op jit(solution)/shard_map/dot_general | solution.py:47
  57.5 0.1 collective-permute-start.1
  57.6 2.0 %collective-permute-done.1 = f32[256,512]{0,1:T(8,128)S(1)} collective-permute-done((f32[256,512]{0,1:T(8,128)}, f32[256,512]{0,1:T(8,128)S(1)}, u32[]{:S(2)}, u32[]{:S(2)}) %collective-permute-start.1) | collective-permute-done | bytes 524320 | tf_op jit(solution)/shard_map/ppermute | solution.py:15
  59.6 0.1 maximum_select_fusion
  59.7 0.1 slice_select_fusion.4
  59.8 1.8 %collective-permute-start.2 = (f32[256,512]{0,1:T(8,128)S(1)}, f32[256,512]{0,1:T(8,128)S(1)}, u32[]{:S(2)}, u32[]{:S(2)}) collective-permute-start(f32[256,512]{0,1:T(8,128)S(1)} %slice_select_fusion.4), channel_id=1, source_target_pairs={{0,8},{8,0},{4,12},{12,4},{16,24},{24,16},{20,28},{28,20},{32,40},... | collective-permute-start | bytes 1572872 | tf_op jit(solution)/shard_map/ppermute | solution.py:15
  61.6 12.4 %collective-permute-done.2 = f32[256,512]{0,1:T(8,128)S(1)} collective-permute-done((f32[256,512]{0,1:T(8,128)S(1)}, f32[256,512]{0,1:T(8,128)S(1)}, u32[]{:S(2)}, u32[]{:S(2)}) %collective-permute-start.2) | collective-permute-done | bytes 524320 | tf_op jit(solution)/shard_map/ppermute | solution.py:15
  74.0 0.6 convolution_add_fusion.1
  74.6 1.8 %fusion.10 = f32[256,512]{1,0:T(8,128)S(1)} fusion(f32[256,512]{0,1:T(8,128)S(1)} %convolution_add_fusion.1, f32[3,256,256]{2,1,0:T(8,128)} %param.9), kind=kOutput, calls=%fused_computation.39 | convolution fusion | flops 403046400 | bytes 1310720 | tf_op jit(solution)/shard_map/kb,kn->bn/dot_general | solution.py:46
  76.5 0.2 copy.9
  76.7 2.1 %broadcast_select_fusion.1 = (f32[256,512]{0,1:T(8,128)}, f32[256,512]{0,1:T(8,128)}, f32[256,512]{0,1:T(8,128)}) fusion(pred[]{:T(512)S(6)} %eq.99, f32[256,512]{0,1:T(8,128)S(1)} %copy.9, f32[256,512]{0,1:T(8,128)S(1)} %collective-permute-done.2, f32[256,1024]{0,1:T(8,128)S(1)} %maximum_select_fusion, f32[256,512]{1,0:T(8,128)S(1)} %fusion.10, ...), kind=kOutput, calls=%fused_computation.58 | convolution fusion | flops 403439616 | bytes 4456449 | tf_op jit(solution)/shard_map/dot_general | solution.py:47
  78.8 1.5 collective-permute-start.3
  80.3 11.8 %collective-permute-done.3 = f32[256,512]{0,1:T(8,128)S(1)} collective-permute-done((f32[256,512]{0,1:T(8,128)}, f32[256,512]{0,1:T(8,128)S(1)}, u32[]{:S(2)}, u32[]{:S(2)}) %collective-permute-start.3) | collective-permute-done | bytes 524320 | tf_op jit(solution)/shard_map/ppermute | solution.py:15
  92.1 1.3 maximum_select_fusion.1
  93.4 0.1 slice_select_fusion.1
  93.5 2.6 %collective-permute-start.4 = (f32[256,512]{0,1:T(8,128)S(1)}, f32[256,512]{0,1:T(8,128)S(1)}, u32[]{:S(2)}, u32[]{:S(2)}) collective-permute-start(f32[256,512]{0,1:T(8,128)S(1)} %slice_select_fusion.1), channel_id=1, source_target_pairs={{0,16},{16,0},{4,20},{20,4},{8,24},{24,8},{12,28},{28,12},{32,48},... | collective-permute-start | bytes 1572872 | tf_op jit(solution)/shard_map/ppermute | solution.py:15
  96.1 21.8 %collective-permute-done.4 = f32[256,512]{0,1:T(8,128)S(1)} collective-permute-done((f32[256,512]{0,1:T(8,128)S(1)}, f32[256,512]{0,1:T(8,128)S(1)}, u32[]{:S(2)}, u32[]{:S(2)}) %collective-permute-start.4) | collective-permute-done | bytes 524320 | tf_op jit(solution)/shard_map/ppermute | solution.py:15
  118.0 0.6 convolution_add_fusion
  118.6 1.8 %fusion.7 = f32[256,512]{1,0:T(8,128)S(1)} fusion(f32[256,512]{0,1:T(8,128)S(1)} %convolution_add_fusion, f32[3,256,256]{2,1,0:T(8,128)} %param.9), kind=kOutput, calls=%fused_computation.33 | convolution fusion | flops 403046400 | bytes 1310720 | tf_op jit(solution)/shard_map/kb,kn->bn/dot_general | solution.py:46
  120.4 0.2 copy.11
  120.6 1.0 broadcast_select_fusion.2
  121.7 0.0 slice-start
  121.7 0.1 collective-permute-start.5
  121.8 25.0 %collective-permute-done.5 = f32[256,512]{0,1:T(8,128)S(1)} collective-permute-done((f32[256,512]{0,1:T(8,128)S(1)}, f32[256,512]{0,1:T(8,128)S(1)}, u32[]{:S(2)}, u32[]{:S(2)}) %collective-permute-start.5) | collective-permute-done | bytes 524320 | tf_op jit(solution)/shard_map/ppermute | solution.py:15
  146.8 0.1 maximum_select_fusion.2
  146.9 0.0 slice-done
  146.9 2.6 %pad_maximum_fusion = f32[1024,1024]{0,1:T(8,128)} fusion(f32[768,1024]{0,1:T(8,128)S(1)} %slice-done, f32[256,1024]{0,1:T(8,128)S(1)} %maximum_select_fusion.2), kind=kLoop, calls=%fused_computation | loop fusion | flops 1048576 | bytes 8388608 | tf_op jit(solution)/shard_map/concatenate | solution.py:81
  149.5 5.3 %copy.13 = f32[1024,1024]{1,0:T(8,128)} copy(f32[1024,1024]{0,1:T(8,128)} %pad_maximum_fusion) | data formatting | bytes 8388608 | tf_op jit(solution)/shard_map/concatenate | solution.py:81
  (3 shorter events, 0.0 us)
Async XLA Ops:
  6.5 32.1 %all-gather.2.cloned.1.call-start = ((), (), s32[]{:S(2)}) async-start(), calls=%async_computation | async-start | bytes 1310720 | tf_op jit(solution)/shard_map/all_gather | solution.py:55
  12.6 32.1 %copy-start.4 = (f32[256,256]{1,0:T(8,128)S(1)}, f32[256,256]{1,0:T(8,128)}, u32[]{:S(2)}) copy-start(f32[256,256]{1,0:T(8,128)} %param.7) | copy-start | bytes 786436
  38.7 7.1 %copy-start.1 = (f32[1024,1024]{0,1:T(8,128)S(1)}, f32[1024,1024]{0,1:T(8,128)}, u32[]{:S(2)}) copy-start(f32[1024,1024]{0,1:T(8,128)} %copy.6) | copy-start | bytes 12582916
  38.7 7.1 %copy-start.2 = (f32[1024,256]{1,0:T(8,128)S(1)}, f32[1024,256]{1,0:T(8,128)}, u32[]{:S(2)}) copy-start(f32[1024,256]{1,0:T(8,128)} %all-gather.2.cloned.1.call-done) | copy-start | bytes 3145732
  45.8 6.0 %copy-start.3 = (f32[3,256,256]{2,1,0:T(8,128)S(1)}, f32[3,256,256]{2,1,0:T(8,128)}, u32[]{:S(2)}) copy-start(f32[3,256,256]{2,1,0:T(8,128)} %param.8) | copy-start | bytes 2359300
  49.6 2.1 %copy-start = (f32[1024,1024]{0,1:T(8,128)}, f32[1024,1024]{0,1:T(8,128)S(1)}, u32[]{:S(2)}) copy-start(f32[1024,1024]{0,1:T(8,128)S(1)} %convolution_subtract_fusion) | copy-start | bytes 12582916
  49.8 2.0 %collective-permute-start = (f32[256,512]{0,1:T(8,128)S(1)}, f32[256,512]{0,1:T(8,128)S(1)}, u32[]{:S(2)}, u32[]{:S(2)}) collective-permute-start(f32[256,512]{0,1:T(8,128)S(1)} %slice_select_fusion.7), channel_id=1, source_target_pairs={{0,4},{4,0},{8,12},{12,8},{16,20},{20,16},{24,28},{28,24},{32,36},... | collective-permute-start | bytes 1572872 | tf_op jit(solution)/shard_map/ppermute | solution.py:15
  57.5 2.1 %collective-permute-start.1 = (f32[256,512]{0,1:T(8,128)}, f32[256,512]{0,1:T(8,128)S(1)}, u32[]{:S(2)}, u32[]{:S(2)}) collective-permute-start(f32[256,512]{0,1:T(8,128)} %get-tuple-element.9), channel_id=1, source_target_pairs={{0,4},{4,0},{8,12},{12,8},{16,20},{20,16},{24,28},{28,24},{32,36},... | collective-permute-start | bytes 1572872 | tf_op jit(solution)/shard_map/ppermute | solution.py:15
  59.8 14.2 %collective-permute-start.2 = (f32[256,512]{0,1:T(8,128)S(1)}, f32[256,512]{0,1:T(8,128)S(1)}, u32[]{:S(2)}, u32[]{:S(2)}) collective-permute-start(f32[256,512]{0,1:T(8,128)S(1)} %slice_select_fusion.4), channel_id=1, source_target_pairs={{0,8},{8,0},{4,12},{12,4},{16,24},{24,16},{20,28},{28,20},{32,40},... | collective-permute-start | bytes 1572872 | tf_op jit(solution)/shard_map/ppermute | solution.py:15
  78.8 13.3 %collective-permute-start.3 = (f32[256,512]{0,1:T(8,128)}, f32[256,512]{0,1:T(8,128)S(1)}, u32[]{:S(2)}, u32[]{:S(2)}) collective-permute-start(f32[256,512]{0,1:T(8,128)} %get-tuple-element.7), channel_id=1, source_target_pairs={{0,8},{8,0},{4,12},{12,4},{16,24},{24,16},{20,28},{28,20},{32,40},... | collective-permute-start | bytes 1572872 | tf_op jit(solution)/shard_map/ppermute | solution.py:15
  93.5 24.5 %collective-permute-start.4 = (f32[256,512]{0,1:T(8,128)S(1)}, f32[256,512]{0,1:T(8,128)S(1)}, u32[]{:S(2)}, u32[]{:S(2)}) collective-permute-start(f32[256,512]{0,1:T(8,128)S(1)} %slice_select_fusion.1), channel_id=1, source_target_pairs={{0,16},{16,0},{4,20},{20,4},{8,24},{24,8},{12,28},{28,12},{32,48},... | collective-permute-start | bytes 1572872 | tf_op jit(solution)/shard_map/ppermute | solution.py:15
  121.7 25.2 %slice-start = ((f32[1024,1024]{0,1:T(8,128)}), f32[768,1024]{0,1:T(8,128)S(1)}, s32[]{:S(2)}) async-start(f32[1024,1024]{0,1:T(8,128)} %copy-done), calls=%async_computation.1 | async-start | bytes 6291456 | tf_op jit(solution)/shard_map/slice | solution.py:61
  121.7 25.1 %collective-permute-start.5 = (f32[256,512]{0,1:T(8,128)S(1)}, f32[256,512]{0,1:T(8,128)S(1)}, u32[]{:S(2)}, u32[]{:S(2)}) collective-permute-start(f32[256,512]{0,1:T(8,128)S(1)} %get-tuple-element.5), channel_id=1, source_target_pairs={{0,16},{16,0},{4,20},{20,4},{8,24},{24,8},{12,28},{28,12},{32,48},... | collective-permute-start | bytes 1572872 | tf_op jit(solution)/shard_map/ppermute | solution.py:15
Sparse Core Ops, SparseCore 0:
  9.1 29.4 all-gather.1
where the time goes:
time: 162 us
  waiting for transfers between devices  102 us (63%)
  matrix products  24.4 us (15%)
  between operations  13.6 us (8%)
  local copies, waits for them, and re-layouts  11.3 us (7%)
  starting transfers between devices  6.33 us (4%)
  other arithmetic  4.38 us (3%)
    ppermute x6, waiting for transfers between devices, from_partner(): return lax.ppermute(block, axis, route)  74.9 us
    all_gather x1, waiting for transfers between devices, per_device(): gathered = lax.all_gather(panel_y, 'col', axis=0, tiled=True)  26.1 us
    ppermute x6, starting transfers between devices, from_partner(): return lax.ppermute(block, axis, route)  6.32 us
    dot_general x3, matrix products, pair_update(): return (first - factor, second - jnp.dot(vees, factor, precision=highest))  6.15 us
    dot_general x1, matrix products, per_device(): proj = jnp.einsum('mb,mn->bn', lower, trailing, precision=highest)  6.04 us
    dot_general x3, matrix products, pair_update(): factor = jnp.einsum('kb,kn->bn', tees, summed, precision=highest)  5.51 us
    unnamed x11, local copies, waits for them, and re-layouts  5.37 us
    concatenate x1, local copies, waits for them, and re-layouts, per_device(): return jnp.concatenate([top, rest], axis=0)  5.34 us
  transfers between devices with their start and end apart: 7, of which 7 were waited for; matrix products, arithmetic and copies ran while one was open for 3% of the time, Pallas kernels for 0%

commit v1 on v0

--- a/solution.py
+++ b/solution.py
@@ -52,7 +52,9 @@
     width = panel_t.shape[1]
     columns = trailing.shape[1]
     half = columns // 2
-    gathered = lax.all_gather(panel_y, "col", axis=0, tiled=True)
+    gathered = jnp.concatenate(
+        lax.all_to_all(jnp.stack([panel_y for _ in range(lax.axis_size("col"))], 0), "col", 0, 0), 0
+    )
     lower = unit_lower(gathered)
     proj = jnp.einsum("mb,mn->bn", lower, trailing, precision=highest)
     weight = jnp.einsum("kb,kn->bn", triangle_factor(panel_t), proj, precision=highest)

time: 162 us -> 139 us (0.86)
  waiting for transfers between devices: 102 us -> 84.6 us
  between operations: 13.6 us -> 0.22 us
  starting transfers between devices: 6.33 us -> 11.9 us
  local copies, waits for them, and re-layouts: 11.3 us -> 13.3 us
    all_gather x1 -> x0, waiting for transfers between devices: 26.1 us -> none  [per_device(): gathered = lax.all_gather(panel_y, 'col', axis=0, tiled=True)]
    all_to_all x0 -> x1, waiting for transfers between devices: none -> 9.75 us  [per_device(): lax.all_to_all(jnp.stack([panel_y for _ in range(lax.axis_size('col'))],...]
    all_to_all x0 -> x1, starting transfers between devices: none -> 4.29 us  [per_device(): lax.all_to_all(jnp.stack([panel_y for _ in range(lax.axis_size('col'))],...]
    another operation x0 -> x1, local copies, waits for them, and re-layouts: none -> 2.01 us  [per_device(): jnp.stack([panel_y for _ in range(lax.axis_size('col'))], 0)]
    unnamed x11 -> x9, local copies, waits for them, and re-layouts: 5.37 us -> 5.36 us
  transfers between devices with their start and end apart: 7 -> 7, of which waited for: 7 -> 7; matrix products, arithmetic and copies ran while one was open for 3% -> 4% of each run, Pallas kernels for 0% -> 0%
where the time goes in v1:
time: 139 us
  waiting for transfers between devices  84.6 us (61%)
  matrix products  24.3 us (17%)
  local copies, waits for them, and re-layouts  13.3 us (10%)
  starting transfers between devices  11.9 us (9%)
  other arithmetic  4.46 us (3%)
    ppermute x6, waiting for transfers between devices, from_partner(): return lax.ppermute(block, axis, route)  74.9 us
    all_to_all x1, waiting for transfers between devices, per_device(): lax.all_to_all(jnp.stack([panel_y for _ in range(lax.axis_size('col'))],...  9.75 us
    ppermute x6, starting transfers between devices, from_partner(): return lax.ppermute(block, axis, route)  7.6 us
    dot_general x3, matrix products, pair_update(): return (first - factor, second - jnp.dot(vees, factor, precision=highest))  6.13 us
    dot_general x1, matrix products, per_device(): proj = jnp.einsum('mb,mn->bn', lower, trailing, precision=highest)  6 us
    dot_general x3, matrix products, pair_update(): factor = jnp.einsum('kb,kn->bn', tees, summed, precision=highest)  5.51 us
    unnamed x9, local copies, waits for them, and re-layouts  5.36 us
    concatenate x1, local copies, waits for them, and re-layouts, per_device(): return jnp.concatenate([top, rest], axis=0)  5.34 us
  transfers between devices with their start and end apart: 7, of which 7 were waited for; matrix products, arithmetic and copies ran while one was open for 4% of the time, Pallas kernels for 0%

profile of v1, /device:TPU:8, one launch (start us, length us, event | category | flops | bytes accessed | tf_op | source)
XLA Modules:
  0.0 138.8 jit_solution(10681230479417532072)
XLA Ops:
  0.0 2.0 %stack.2 = f32[4,256,256]{2,1,0:T(8,128)} broadcast(f32[256,256]{1,0:T(8,128)} %param.6), dimensions={1,2} | broadcast | bytes 1310720 | tf_op jit(solution)/shard_map/stack | solution.py:56
  2.0 4.3 %all-to-all-start = ((f32[4,256,256]{2,1,0:T(8,128)}), f32[4,256,256]{2,1,0:T(8,128)S(1)}, u32[]{:S(2)}, u32[]{:S(2)}) async-start(f32[4,256,256]{2,1,0:T(8,128)} %stack.2), calls=%async_computation | async-start | bytes 2097152 | tf_op jit(solution)/shard_map/all_to_all | solution.py:56
  6.3 5.3 %copy.6 = f32[1024,1024]{0,1:T(8,128)} copy(f32[1024,1024]{1,0:T(8,128)} %param.5) | data formatting | bytes 8388608 | tf_op args[0]
  11.6 9.8 %all-to-all-done = f32[4,256,256]{2,1,0:T(8,128)S(1)} async-done(((f32[4,256,256]{2,1,0:T(8,128)}), f32[4,256,256]{2,1,0:T(8,128)S(1)}, u32[]{:S(2)}, u32[]{:S(2)}) %all-to-all-start) | async-done | bytes 1048608 | tf_op jit(solution)/shard_map/all_to_all | solution.py:56
  21.4 0.1 bitcast_select_fusion
  21.5 0.0 copy-start.1
  21.5 6.0 %fusion.59 = f32[256,1024]{1,0:T(8,128)S(1)} fusion(f32[1024,256]{1,0:T(8,128)S(1)} %bitcast_select_fusion, f32[1024,1024]{1,0:T(8,128)} %param.5), kind=kOutput, calls=%fused_computation.94 | convolution fusion | flops 3221225472 | bytes 6291456 | tf_op jit(solution)/shard_map/mb,mn->bn/dot_general | solution.py:59
  27.5 0.0 copy-done.3
  27.5 1.1 fusion.12
  28.6 0.0 copy-done.1
  28.6 0.0 copy-start.2
  28.6 3.8 %convolution_subtract_fusion = f32[1024,1024]{0,1:T(8,128)S(1)} fusion(f32[1024,1024]{0,1:T(8,128)S(1)} %copy-done.1, f32[1024,256]{1,0:T(8,128)S(1)} %bitcast_select_fusion, f32[256,1024]{1,0:T(8,128)S(1)} %fusion.12), kind=kOutput, calls=%fused_computation.1 | convolution fusion | flops 3222274048 | bytes 10485760 | tf_op jit(solution)/shard_map/dot_general | solution.py:61
  32.4 0.0 copy-start
  32.4 0.1 slice_select_fusion.7
  32.5 0.1 collective-permute-start
  32.6 1.9 %collective-permute-done = f32[256,512]{0,1:T(8,128)S(1)} collective-permute-done((f32[256,512]{0,1:T(8,128)S(1)}, f32[256,512]{0,1:T(8,128)S(1)}, u32[]{:S(2)}, u32[]{:S(2)}) %collective-permute-start) | collective-permute-done | bytes 524320 | tf_op jit(solution)/shard_map/ppermute | solution.py:15
  34.5 0.0 copy-done
  34.5 0.6 convolution_add_fusion.2
  35.1 1.8 %fusion.8 = f32[256,512]{1,0:T(8,128)S(1)} fusion(f32[256,512]{0,1:T(8,128)S(1)} %convolution_add_fusion.2, f32[3,256,256]{2,1,0:T(8,128)} %param.9), kind=kOutput, calls=%fused_computation.40 | convolution fusion | flops 403046400 | bytes 1310720 | tf_op jit(solution)/shard_map/kb,kn->bn/dot_general | solution.py:46
  37.0 0.2 copy.7
  37.2 3.0 %broadcast_select_fusion = (f32[256,512]{0,1:T(8,128)}, f32[256,512]{0,1:T(8,128)S(1)}, f32[256,512]{0,1:T(8,128)S(1)}) fusion(pred[]{:T(512)S(6)} %eq.100, f32[256,512]{0,1:T(8,128)S(1)} %copy.7, f32[256,512]{0,1:T(8,128)S(1)} %collective-permute-done, f32[1024,1024]{0,1:T(8,128)} %copy-done, f32[256,512]{1,0:T(8,128)S(1)} %fusion.8, ...), kind=kOutput, calls=%fused_computation.52 | convolution fusion | flops 403439616 | bytes 4456449 | tf_op jit(solution)/shard_map/dot_general | solution.py:47
  40.2 0.1 collective-permute-start.1
  40.3 2.0 %collective-permute-done.1 = f32[256,512]{0,1:T(8,128)S(1)} collective-permute-done((f32[256,512]{0,1:T(8,128)}, f32[256,512]{0,1:T(8,128)S(1)}, u32[]{:S(2)}, u32[]{:S(2)}) %collective-permute-start.1) | collective-permute-done | bytes 524320 | tf_op jit(solution)/shard_map/ppermute | solution.py:15
  42.3 0.1 maximum_select_fusion
  42.4 0.1 slice_select_fusion.4
  42.5 2.2 %collective-permute-start.2 = (f32[256,512]{0,1:T(8,128)S(1)}, f32[256,512]{0,1:T(8,128)S(1)}, u32[]{:S(2)}, u32[]{:S(2)}) collective-permute-start(f32[256,512]{0,1:T(8,128)S(1)} %slice_select_fusion.4), channel_id=1, source_target_pairs={{0,8},{8,0},{4,12},{12,4},{16,24},{24,16},{20,28},{28,20},{32,40},... | collective-permute-start | bytes 1572872 | tf_op jit(solution)/shard_map/ppermute | solution.py:15
  44.7 12.2 %collective-permute-done.2 = f32[256,512]{0,1:T(8,128)S(1)} collective-permute-done((f32[256,512]{0,1:T(8,128)S(1)}, f32[256,512]{0,1:T(8,128)S(1)}, u32[]{:S(2)}, u32[]{:S(2)}) %collective-permute-start.2) | collective-permute-done | bytes 524320 | tf_op jit(solution)/shard_map/ppermute | solution.py:15
  56.9 0.6 convolution_add_fusion.1
  57.5 1.8 %fusion.5 = f32[256,512]{1,0:T(8,128)S(1)} fusion(f32[256,512]{0,1:T(8,128)S(1)} %convolution_add_fusion.1, f32[3,256,256]{2,1,0:T(8,128)} %param.9), kind=kOutput, calls=%fused_computation.34 | convolution fusion | flops 403046400 | bytes 1310720 | tf_op jit(solution)/shard_map/kb,kn->bn/dot_general | solution.py:46
  59.4 0.2 copy.9
  59.6 2.1 %broadcast_select_fusion.1 = (f32[256,512]{0,1:T(8,128)}, f32[256,512]{0,1:T(8,128)}, f32[256,512]{0,1:T(8,128)}) fusion(pred[]{:T(512)S(6)} %eq.99, f32[256,512]{0,1:T(8,128)S(1)} %copy.9, f32[256,512]{0,1:T(8,128)S(1)} %collective-permute-done.2, f32[256,1024]{0,1:T(8,128)S(1)} %maximum_select_fusion, f32[256,512]{1,0:T(8,128)S(1)} %fusion.5, ...), kind=kOutput, calls=%fused_computation.53 | convolution fusion | flops 403439616 | bytes 4456449 | tf_op jit(solution)/shard_map/dot_general | solution.py:47
  61.7 1.7 %collective-permute-start.3 = (f32[256,512]{0,1:T(8,128)}, f32[256,512]{0,1:T(8,128)S(1)}, u32[]{:S(2)}, u32[]{:S(2)}) collective-permute-start(f32[256,512]{0,1:T(8,128)} %get-tuple-element.7), channel_id=1, source_target_pairs={{0,8},{8,0},{4,12},{12,4},{16,24},{24,16},{20,28},{28,20},{32,40},... | collective-permute-start | bytes 1572872 | tf_op jit(solution)/shard_map/ppermute | solution.py:15
  63.4 11.7 %collective-permute-done.3 = f32[256,512]{0,1:T(8,128)S(1)} collective-permute-done((f32[256,512]{0,1:T(8,128)}, f32[256,512]{0,1:T(8,128)S(1)}, u32[]{:S(2)}, u32[]{:S(2)}) %collective-permute-start.3) | collective-permute-done | bytes 524320 | tf_op jit(solution)/shard_map/ppermute | solution.py:15
  75.2 1.3 maximum_select_fusion.1
  76.5 0.1 slice_select_fusion.1
  76.5 3.4 %collective-permute-start.4 = (f32[256,512]{0,1:T(8,128)S(1)}, f32[256,512]{0,1:T(8,128)S(1)}, u32[]{:S(2)}, u32[]{:S(2)}) collective-permute-start(f32[256,512]{0,1:T(8,128)S(1)} %slice_select_fusion.1), channel_id=1, source_target_pairs={{0,16},{16,0},{4,20},{20,4},{8,24},{24,8},{12,28},{28,12},{32,48},... | collective-permute-start | bytes 1572872 | tf_op jit(solution)/shard_map/ppermute | solution.py:15
  79.9 21.9 %collective-permute-done.4 = f32[256,512]{0,1:T(8,128)S(1)} collective-permute-done((f32[256,512]{0,1:T(8,128)S(1)}, f32[256,512]{0,1:T(8,128)S(1)}, u32[]{:S(2)}, u32[]{:S(2)}) %collective-permute-start.4) | collective-permute-done | bytes 524320 | tf_op jit(solution)/shard_map/ppermute | solution.py:15
  101.8 0.6 convolution_add_fusion
  102.4 1.8 %fusion.2 = f32[256,512]{1,0:T(8,128)S(1)} fusion(f32[256,512]{0,1:T(8,128)S(1)} %convolution_add_fusion, f32[3,256,256]{2,1,0:T(8,128)} %param.9), kind=kOutput, calls=%fused_computation.28 | convolution fusion | flops 403046400 | bytes 1310720 | tf_op jit(solution)/shard_map/kb,kn->bn/dot_general | solution.py:46
  104.3 0.2 copy.11
  104.5 1.0 broadcast_select_fusion.2
  105.5 0.0 slice-start
  105.5 0.1 collective-permute-start.5
  105.6 25.1 %collective-permute-done.5 = f32[256,512]{0,1:T(8,128)S(1)} collective-permute-done((f32[256,512]{0,1:T(8,128)S(1)}, f32[256,512]{0,1:T(8,128)S(1)}, u32[]{:S(2)}, u32[]{:S(2)}) %collective-permute-start.5) | collective-permute-done | bytes 524320 | tf_op jit(solution)/shard_map/ppermute | solution.py:15
  130.7 0.1 maximum_select_fusion.2
  130.9 0.0 slice-done
  130.9 2.6 %pad_maximum_fusion = f32[1024,1024]{0,1:T(8,128)} fusion(f32[768,1024]{0,1:T(8,128)S(1)} %slice-done, f32[256,1024]{0,1:T(8,128)S(1)} %maximum_select_fusion.2), kind=kLoop, calls=%fused_computation | loop fusion | flops 1048576 | bytes 8388608 | tf_op jit(solution)/shard_map/concatenate | solution.py:83
  133.5 5.3 %copy.13 = f32[1024,1024]{1,0:T(8,128)} copy(f32[1024,1024]{0,1:T(8,128)} %pad_maximum_fusion) | data formatting | bytes 8388608 | tf_op jit(solution)/shard_map/concatenate | solution.py:83
  (2 shorter events, 0.0 us)
Async XLA Ops:
  2.0 19.4 %all-to-all-start = ((f32[4,256,256]{2,1,0:T(8,128)}), f32[4,256,256]{2,1,0:T(8,128)S(1)}, u32[]{:S(2)}, u32[]{:S(2)}) async-start(f32[4,256,256]{2,1,0:T(8,128)} %stack.2), calls=%async_computation | async-start | bytes 2097152 | tf_op jit(solution)/shard_map/all_to_all | solution.py:56
  11.6 15.9 %copy-start.3 = (f32[256,256]{1,0:T(8,128)S(1)}, f32[256,256]{1,0:T(8,128)}, u32[]{:S(2)}) copy-start(f32[256,256]{1,0:T(8,128)} %param.7) | copy-start | bytes 786436
  21.5 7.1 %copy-start.1 = (f32[1024,1024]{0,1:T(8,128)S(1)}, f32[1024,1024]{0,1:T(8,128)}, u32[]{:S(2)}) copy-start(f32[1024,1024]{0,1:T(8,128)} %copy.6) | copy-start | bytes 12582916
  28.6 5.9 %copy-start.2 = (f32[3,256,256]{2,1,0:T(8,128)S(1)}, f32[3,256,256]{2,1,0:T(8,128)}, u32[]{:S(2)}) copy-start(f32[3,256,256]{2,1,0:T(8,128)} %param.8) | copy-start | bytes 2359300
  32.4 2.1 %copy-start = (f32[1024,1024]{0,1:T(8,128)}, f32[1024,1024]{0,1:T(8,128)S(1)}, u32[]{:S(2)}) copy-start(f32[1024,1024]{0,1:T(8,128)S(1)} %convolution_subtract_fusion) | copy-start | bytes 12582916
  32.5 2.0 %collective-permute-start = (f32[256,512]{0,1:T(8,128)S(1)}, f32[256,512]{0,1:T(8,128)S(1)}, u32[]{:S(2)}, u32[]{:S(2)}) collective-permute-start(f32[256,512]{0,1:T(8,128)S(1)} %slice_select_fusion.7), channel_id=1, source_target_pairs={{0,4},{4,0},{8,12},{12,8},{16,20},{20,16},{24,28},{28,24},{32,36},... | collective-permute-start | bytes 1572872 | tf_op jit(solution)/shard_map/ppermute | solution.py:15
  40.2 2.1 %collective-permute-start.1 = (f32[256,512]{0,1:T(8,128)}, f32[256,512]{0,1:T(8,128)S(1)}, u32[]{:S(2)}, u32[]{:S(2)}) collective-permute-start(f32[256,512]{0,1:T(8,128)} %get-tuple-element.9), channel_id=1, source_target_pairs={{0,4},{4,0},{8,12},{12,8},{16,20},{20,16},{24,28},{28,24},{32,36},... | collective-permute-start | bytes 1572872 | tf_op jit(solution)/shard_map/ppermute | solution.py:15
  42.5 14.4 %collective-permute-start.2 = (f32[256,512]{0,1:T(8,128)S(1)}, f32[256,512]{0,1:T(8,128)S(1)}, u32[]{:S(2)}, u32[]{:S(2)}) collective-permute-start(f32[256,512]{0,1:T(8,128)S(1)} %slice_select_fusion.4), channel_id=1, source_target_pairs={{0,8},{8,0},{4,12},{12,4},{16,24},{24,16},{20,28},{28,20},{32,40},... | collective-permute-start | bytes 1572872 | tf_op jit(solution)/shard_map/ppermute | solution.py:15
  61.7 13.5 %collective-permute-start.3 = (f32[256,512]{0,1:T(8,128)}, f32[256,512]{0,1:T(8,128)S(1)}, u32[]{:S(2)}, u32[]{:S(2)}) collective-permute-start(f32[256,512]{0,1:T(8,128)} %get-tuple-element.7), channel_id=1, source_target_pairs={{0,8},{8,0},{4,12},{12,4},{16,24},{24,16},{20,28},{28,20},{32,40},... | collective-permute-start | bytes 1572872 | tf_op jit(solution)/shard_map/ppermute | solution.py:15
  76.5 25.3 %collective-permute-start.4 = (f32[256,512]{0,1:T(8,128)S(1)}, f32[256,512]{0,1:T(8,128)S(1)}, u32[]{:S(2)}, u32[]{:S(2)}) collective-permute-start(f32[256,512]{0,1:T(8,128)S(1)} %slice_select_fusion.1), channel_id=1, source_target_pairs={{0,16},{16,0},{4,20},{20,4},{8,24},{24,8},{12,28},{28,12},{32,48},... | collective-permute-start | bytes 1572872 | tf_op jit(solution)/shard_map/ppermute | solution.py:15
  105.5 25.3 %slice-start = ((f32[1024,1024]{0,1:T(8,128)}), f32[768,1024]{0,1:T(8,128)S(1)}, s32[]{:S(2)}) async-start(f32[1024,1024]{0,1:T(8,128)} %copy-done), calls=%async_computation.1 | async-start | bytes 6291456 | tf_op jit(solution)/shard_map/slice | solution.py:63
  105.5 25.2 %collective-permute-start.5 = (f32[256,512]{0,1:T(8,128)S(1)}, f32[256,512]{0,1:T(8,128)S(1)}, u32[]{:S(2)}, u32[]{:S(2)}) collective-permute-start(f32[256,512]{0,1:T(8,128)S(1)} %get-tuple-element.5), channel_id=1, source_target_pairs={{0,16},{16,0},{4,20},{20,4},{8,24},{24,8},{12,28},{28,12},{32,48},... | collective-permute-start | bytes 1572872 | tf_op jit(solution)/shard_map/ppermute | solution.py:15
